TPU v7x, 32 devices: a whole 2x2x4 slice. The times are simulated.
32 devices in a mesh: ckpt: 2 (over y), row: 16 (over z, x, core).
Axes of the slice: x: 2, y: 2, z: 4, core: 2. Of those that a mesh axis runs over, the one named last changes fastest.
Arguments:
- activations: bfloat16 [4096, 4096], P(('ckpt', 'row')), parts along dimension 0, may hold values from -6 to 6
- gate_pre: bfloat16 [4096, 7168], P(('ckpt', 'row')), parts along dimension 0, may hold values from -8 to 8
- out_grad: bfloat16 [4096, 4096], P(('ckpt', 'row')), parts along dimension 0, may hold values from -6 to 6
- down_weight: bfloat16 [14336, 4096], P(('ckpt', 'row')), parts along dimension 0, may hold values from -0.09375 to 0.09375
- proj_in: bfloat16 [4096, 64], replicated, may hold values from -0.09375 to 0.09375
- proj_out: bfloat16 [7168, 64], replicated, may hold values from -0.0625 to 0.0625
- stored: bfloat16 [24576, 4096], P(('ckpt', 'row')), parts along dimension 0, may hold values from -0.09375 to 0.09375
- visible: int32 [16], replicated, may hold values from 1 to 12288, as said below
Outputs:
- scores: float32 [32, 12288], P('ckpt', 'row'), parts along dimension 0
There are 2 independent parts, one for each index of `ckpt`. A program takes and returns all parts, laid end to end along the dimension named above; an argument that names none is the same for every part. Nothing has to cross between parts.
Inputs may be any that keep to these rules, and one draw needn't show every extreme that they name: `visible`: some query example sees all 12288 stored examples and some sees exactly one.
All inputs are finite; a program needn't handle non-finite values.
Results may differ from a plain program's by a relative error of at most 0.0064.
Values may be sent and summed in bfloat16 or wider, within the bound.
No kernel may reach another device: no remote copies, remote signals or barrier semaphores. Data moves between devices by JAX's collectives and lax.ppermute only.
A program may use at most 128 MiB of HBM per device.

v0:
```python
import jax
import jax.numpy as jnp
from jax import lax
from jax.sharding import PartitionSpec as P

SEQ_LEN = 128


def partner(value, axis, bit):
    return lax.ppermute(value, axis, [(i, i ^ 1 << bit) for i in range(lax.axis_size(axis))])


def collect(pieces, position, bit_list, sender):
    for bit_level in bit_list:
        partner_rows = sender(pieces, bit_level)
        upper_half = position >> bit_level & 1 == 1
        pieces = jnp.where(
            upper_half,
            jnp.concatenate([partner_rows, pieces], axis=0),
            jnp.concatenate([pieces, partner_rows], axis=0),
        )
    return pieces


def xor_order(slot_data, lane_id, lane_bits):
    lane_total = 1 << lane_bits
    for bit_level in range(lane_bits):
        shaped = slot_data.reshape(
            (lane_total >> bit_level + 1, 2, 1 << bit_level) + slot_data.shape[1:]
        )
        flipped = shaped[:, ::-1].reshape(slot_data.shape)
        slot_data = jnp.where(lane_id >> bit_level & 1 == 1, flipped, slot_data)
    return slot_data


def lane_exchange(slot_data, lane_id, lane_bits):
    lane_total = 1 << lane_bits
    slot_data = xor_order(slot_data, lane_id, lane_bits)
    for bit_level in range(lane_bits):
        shaped = slot_data.reshape(
            (lane_total >> bit_level + 1, 2, 1 << bit_level) + slot_data.shape[1:]
        )
        arrived = partner(shaped[:, 1], "row", bit_level)
        slot_data = jnp.concatenate([shaped[:, :1], arrived[:, None]], axis=1).reshape(
            slot_data.shape
        )
    return xor_order(slot_data, lane_id, lane_bits)


def shards(activations, gate_pre, out_grad, down_weight, proj_in, proj_out, stored, visible):
    devices = lax.axis_size("row")
    position = lax.axis_index("row")
    total_bits = devices.bit_length() - 1
    lane_bits = 3
    lane_total = 1 << lane_bits
    lane_id = position % lane_total
    tokens_dev = activations.shape[0]
    hidden_total = gate_pre.shape[1]
    rows_piece = down_weight.shape[0]
    groups = hidden_total // (rows_piece * lane_total)
    rank_size = proj_in.shape[1]
    weights_lane = collect(
        down_weight,
        position,
        range(lane_bits, total_bits),
        lambda pieces, bit_level: partner(pieces, "row", bit_level),
    )
    grad_group = collect(
        out_grad,
        position,
        range(0, lane_bits),
        lambda pieces, bit_level: partner(pieces, "row", bit_level),
    )
    hidden_block = lax.dot_general(
        grad_group, weights_lane, (((1,), (1,)), ((), ())), preferred_element_type=jnp.float32
    ).astype(jnp.bfloat16)
    received = lane_exchange(
        hidden_block.reshape(lane_total, tokens_dev, groups * rows_piece), lane_id, lane_bits
    )
    full_grad = (
        received.reshape(lane_total, tokens_dev, groups, rows_piece)
        .transpose(1, 2, 0, 3)
        .reshape(tokens_dev, hidden_total)
    )
    up_grad = (
        lax.optimization_barrier(full_grad).astype(jnp.float32)
        * jax.nn.silu(gate_pre.astype(jnp.float32))
    ).astype(jnp.bfloat16)
    out_proj = jnp.dot(up_grad, proj_out, preferred_element_type=jnp.float32).astype(jnp.bfloat16)
    in_proj = jnp.dot(activations, proj_in, preferred_element_type=jnp.float32).astype(jnp.bfloat16)
    examples_dev = tokens_dev // SEQ_LEN
    in_split = in_proj.astype(jnp.float32).reshape(examples_dev, SEQ_LEN, rank_size)
    out_split = out_proj.astype(jnp.float32).reshape(examples_dev, SEQ_LEN, rank_size)
    raw_feature = jnp.einsum(
        "esa,esb->eab", in_split, out_split, preferred_element_type=jnp.float32
    ).reshape(examples_dev, rank_size * rank_size)
    scale = lax.rsqrt(jnp.mean(raw_feature * raw_feature, axis=1, keepdims=True) + 1e-06)
    queries = (raw_feature * scale).astype(jnp.bfloat16)
    stored_rows = stored.shape[0]
    column = position * stored_rows + jnp.arange(stored_rows, dtype=jnp.int32)
    products = lax.dot_general(
        lax.all_gather(queries, "row", axis=0, tiled=True),
        stored,
        (((1,), (1,)), ((), ())),
        preferred_element_type=jnp.float32,
    )
    return jnp.where(column[None, :] < visible[:, None], products, jnp.float32(0.0))


def solution(mesh):
    return jax.shard_map(
        shards,
        mesh=mesh,
        in_specs=(
            P(("ckpt", "row"), None),
            P(("ckpt", "row"), None),
            P(("ckpt", "row"), None),
            P(("ckpt", "row"), None),
            P(),
            P(),
            P(("ckpt", "row"), None),
            P(),
        ),
        out_specs=P("ckpt", "row"),
        check_vma=False,
    )
```

profile of v0, /device:TPU:0, one launch (start us, length us, event | category | flops | bytes accessed | tf_op | source)
XLA Modules:
  0.0 381.6 jit_solution(10606979016936965666)
XLA Ops:
  0.0 0.0 copy-start
  0.0 0.5 collective-permute-start
  0.5 2.6 collective-permute-done
  3.1 3.1 maximum_select_fusion.5
  6.2 2.9 collective-permute-start.1
  9.2 46.0 %collective-permute-done.1 = bf16[256,4096]{1,0:T(8,128)(2,1)} collective-permute-done((bf16[256,4096]{1,0:T(8,128)(2,1)S(1)}, bf16[256,4096]{1,0:T(8,128)(2,1)}, u32[]{:S(2)}, u32[]{:S(2)}) %collective-permute-start.1) | collective-permute-done | bytes 2097184 | tf_op jit(solution)/shard_map/ppermute | solution.py:10
  55.2 4.7 %maximum_select_fusion.4 = bf16[512,4096]{1,0:T(8,128)(2,1)} fusion(bf16[256,4096]{1,0:T(8,128)(2,1)S(1)} %maximum_select_fusion.5, bf16[256,4096]{1,0:T(8,128)(2,1)} %collective-permute-done.1, pred[]{:T(512)S(6)} %eq.30), kind=kLoop, calls=%fused_computation.17 | loop fusion | flops 18874368 | bytes 8388609 | tf_op jit(solution)/shard_map/jit(_where)/select_n | solution.py:17
  59.9 1.8 collective-permute-start.2
  61.8 2.6 collective-permute-start.3
  64.4 165.7 %collective-permute-done.3 = bf16[448,4096]{1,0:T(8,128)(2,1)} collective-permute-done((bf16[448,4096]{1,0:T(8,128)(2,1)}, bf16[448,4096]{1,0:T(8,128)(2,1)}, u32[]{:S(2)}, u32[]{:S(2)}) %collective-permute-start.3) | collective-permute-done | bytes 3670048 | tf_op jit(solution)/shard_map/ppermute | solution.py:10
  230.0 1.0 collective-permute-done.2
  231.0 14.4 %fusion.20 = bf16[1024,896]{1,0:T(8,128)(2,1)S(1)} fusion(bf16[448,4096]{1,0:T(8,128)(2,1)} %param.11, bf16[448,4096]{1,0:T(8,128)(2,1)} %collective-permute-done.3, pred[]{:T(512)S(6)} %eq.32, bf16[512,4096]{1,0:T(8,128)(2,1)} %maximum_select_fusion.4, bf16[512,4096]{1,0:T(8,128)(2,1)} %collective-permute-done.2, pred[]{:T(512)S(6)} %eq.29), kind=kOutput, calls=%fused_computation.35 | convolution fusion | flops 7587889152 | bytes 17563650 | tf_op jit(solution)/shard_map/dot_general | solution.py:74
  245.5 1.5 rev.18
  246.9 3.6 copy.27
  250.5 2.4 copy.28
  252.9 2.9 broadcast_select_fusion
  255.9 2.9 rev.19
  258.8 2.4 copy.30
  261.2 3.0 select_select_fusion.2
  264.2 2.9 rev.20
  267.1 3.6 copy.32
  270.7 3.6 copy.31
  274.3 0.8 select_select_fusion.1
  275.1 1.1 fusion.36
  276.2 0.0 collective-permute-start.4
  276.2 0.6 copy.33
  276.8 2.2 collective-permute-done.4
  279.0 1.6 copy.34
  280.6 0.2 fusion.28
  280.8 3.5 collective-permute-start.5
  284.3 20.7 %collective-permute-done.5 = bf16[2,2,128,896]{2,3,1,0:T(8,128)(2,1)S(1)} collective-permute-done((bf16[2,2,128,896]{2,3,1,0:T(8,128)(2,1)S(1)}, bf16[2,2,128,896]{2,3,1,0:T(8,128)(2,1)S(1)}, u32[]{:S(2)}, u32[]{:S(2)}) %collective-permute-start.5) | collective-permute-done | bytes 917536 | tf_op jit(solution)/shard_map/ppermute | solution.py:10
  304.9 0.2 pad_maximum_fusion
  305.1 1.1 fusion.35
  306.2 0.0 copy-start.1
  306.2 0.0 copy-start.4
  306.2 3.1 collective-permute-start.6
  309.3 3.9 %copy.37 = bf16[128,7168]{0,1:T(8,128)(2,1)} copy(bf16[128,7168]{1,0:T(8,128)(2,1)} %param.9) | data formatting | bytes 3670016 | tf_op args[1]
  313.2 0.0 copy-done
  313.2 0.0 copy-done.4
  313.2 0.5 convolution_convert_fusion
  313.7 15.9 %collective-permute-done.6 = bf16[1,4,128,896]{2,3,1,0:T(8,128)(2,1)S(1)} collective-permute-done((bf16[1,4,128,896]{2,3,1,0:T(8,128)(2,1)}, bf16[1,4,128,896]{2,3,1,0:T(8,128)(2,1)S(1)}, u32[]{:S(2)}, u32[]{:S(2)}) %collective-permute-start.6) | collective-permute-done | bytes 917536 | tf_op jit(solution)/shard_map/ppermute | solution.py:10
  329.7 0.0 copy-start.2
  329.7 0.0 copy-done.1
  329.7 1.6 pad_maximum_fusion.1
  331.3 0.0 copy-done.2
  331.3 1.6 rev.21
  332.9 2.9 maximum_select_fusion.6
  335.9 2.9 rev.22
  338.7 2.9 select_select_fusion
  341.7 2.9 rev.23
  344.6 1.8 select_bitcast_fusion
  346.5 0.0 copy-start.3
  346.5 1.4 copy.36
  347.8 0.8 copy-done.3
  348.6 0.0 copy-start.5
  348.6 4.0 %multiply_reduce_fusion = (f32[]{:T(128)}, f32[64,64]{1,0:T(8,128)S(1)}) fusion(bf16[128,64]{0,1:T(8,128)(2,1)S(1)} %convolution_convert_fusion, bf16[7168,64]{0,1:T(8,128)(2,1)} %param.13, bf16[128,7168]{0,1:T(8,128)(2,1)S(1)} %copy-done.3, bf16[128,7168]{0,1:T(8,128)(2,1)} %bitcast.65), kind=kOutput, calls=%fused_computation.49 | convolution fusion | flops 125845504 | bytes 4620292 | tf_op jit(solution)/shard_map/esa,esb->eab/dot_general | solution.py:94
  353.3 0.1 reshape.191
  353.4 23.0 %all-gather = bf16[16,1,4096]{2,1,0:T(2,128)(2,1)S(1)} all-gather(bf16[1,1,4096]{2,1,0:T(2,128)(2,1)S(1)} %reshape.191), channel_id=1, replica_groups=mesh['ckpt'=2,'row'=16] {'row'}, dimensions={0}, use_global_device_ids=true | all-gather | bytes 139264 | tf_op jit(solution)/shard_map/all_gather | solution.py:102
  376.4 0.0 copy-done.5
  376.4 5.2 %convolution_select_fusion = f32[16,768]{1,0:T(8,128)} fusion(bf16[768,4096]{1,0:T(8,128)(2,1)} %param.14, bf16[16,1,4096]{2,1,0:T(2,128)(2,1)S(1)} %all-gather, s32[768]{0:T(1024)S(1)} %iota_add_fusion, s32[16]{0:T(128)S(1)} %copy-done.5), kind=kOutput, calls=%fused_computation.36 | convolution fusion | flops 100687872 | bytes 6474816 | tf_op jit(solution)/shard_map/dot_general | solution.py:101
  (2 shorter events, 0.0 us)
Async XLA Ops:
  0.0 313.2 %copy-start = (bf16[128,4096]{1,0:T(8,128)(2,1)S(1)}, bf16[128,4096]{1,0:T(8,128)(2,1)}, u32[]{:S(2)}) copy-start(bf16[128,4096]{1,0:T(8,128)(2,1)} %param.8) | copy-start | bytes 3145732
  0.0 3.1 collective-permute-start
  6.2 49.0 %collective-permute-start.1 = (bf16[256,4096]{1,0:T(8,128)(2,1)S(1)}, bf16[256,4096]{1,0:T(8,128)(2,1)}, u32[]{:S(2)}, u32[]{:S(2)}) collective-permute-start(bf16[256,4096]{1,0:T(8,128)(2,1)S(1)} %maximum_select_fusion.5), channel_id=1, source_target_pairs={{0,2},{1,3},{2,0},{3,1},{4,6},{5,7},{6,4},{7,5},{8,10},{9,11},{10,... | collective-permute-start | bytes 6291464 | tf_op jit(solution)/shard_map/ppermute | solution.py:10
  59.9 171.1 %collective-permute-start.2 = (bf16[512,4096]{1,0:T(8,128)(2,1)}, bf16[512,4096]{1,0:T(8,128)(2,1)}, u32[]{:S(2)}, u32[]{:S(2)}) collective-permute-start(bf16[512,4096]{1,0:T(8,128)(2,1)} %maximum_select_fusion.4), channel_id=1, source_target_pairs={{0,4},{1,5},{2,6},{3,7},{4,0},{5,1},{6,2},{7,3},{8,12},{9,13},{10,... | collective-permute-start | bytes 12582920 | tf_op jit(solution)/shard_map/ppermute | solution.py:10
  61.8 168.3 %collective-permute-start.3 = (bf16[448,4096]{1,0:T(8,128)(2,1)}, bf16[448,4096]{1,0:T(8,128)(2,1)}, u32[]{:S(2)}, u32[]{:S(2)}) collective-permute-start(bf16[448,4096]{1,0:T(8,128)(2,1)} %param.11), channel_id=1, source_target_pairs={{0,8},{1,9},{2,10},{3,11},{4,12},{5,13},{6,14},{7,15},{8,0},{9,1},... | collective-permute-start | bytes 11010056 | tf_op jit(solution)/shard_map/ppermute | solution.py:10
  276.2 2.8 collective-permute-start.4
  280.8 24.2 %collective-permute-start.5 = (bf16[2,2,128,896]{2,3,1,0:T(8,128)(2,1)S(1)}, bf16[2,2,128,896]{2,3,1,0:T(8,128)(2,1)S(1)}, u32[]{:S(2)}, u32[]{:S(2)}) collective-permute-start(bf16[2,2,128,896]{2,3,1,0:T(8,128)(2,1)S(1)} %get-tuple-element.8), channel_id=1, source_target_pairs={{0,2},{1,3},{2,0},{3,1},{4,6},{5,7},{6,4},{7,5},{8,10},{9,11},{10,... | collective-permute-start | bytes 2752520 | tf_op jit(solution)/shard_map/ppermute | solution.py:10
  306.2 23.5 %copy-start.1 = (bf16[1,1,4,128,896]{3,4,2,1,0:T(8,128)(2,1)}, bf16[1,1,4,128,896]{3,4,2,1,0:T(8,128)(2,1)S(1)}, u32[]{:S(2)}) copy-start(bf16[1,1,4,128,896]{3,4,2,1,0:T(8,128)(2,1)S(1)} %get-tuple-element.5) | copy-start | bytes 2752516
  306.2 7.1 %copy-start.4 = (bf16[4096,64]{0,1:T(8,128)(2,1)S(1)}, bf16[4096,64]{0,1:T(8,128)(2,1)}, u32[]{:S(2)}) copy-start(bf16[4096,64]{0,1:T(8,128)(2,1)} %param.12) | copy-start | bytes 1572868
  306.2 23.5 %collective-permute-start.6 = (bf16[1,4,128,896]{2,3,1,0:T(8,128)(2,1)}, bf16[1,4,128,896]{2,3,1,0:T(8,128)(2,1)S(1)}, u32[]{:S(2)}, u32[]{:S(2)}) collective-permute-start(bf16[1,4,128,896]{2,3,1,0:T(8,128)(2,1)} %get-tuple-element.6), channel_id=1, source_target_pairs={{0,4},{1,5},{2,6},{3,7},{4,0},{5,1},{6,2},{7,3},{8,12},{9,13},{10,... | collective-permute-start | bytes 2752520 | tf_op jit(solution)/shard_map/ppermute | solution.py:10
  329.7 1.6 copy-start.2
  346.5 2.2 copy-start.3
  348.6 27.8 %copy-start.5 = (s32[16]{0:T(128)S(1)}, s32[16]{0:T(128)}, u32[]{:S(2)}) copy-start(s32[16]{0:T(128)} %param.15) | copy-start | bytes 196
where the time goes:
time: 382 us
  waiting for transfers between devices  254 us (66%)
  local copies, waits for them, and re-layouts  40.9 us (11%)
  other arithmetic  24.3 us (6%)
  matrix products  24 us (6%)
  blocking collectives  23 us (6%)
  starting transfers between devices  14.5 us (4%)
    ppermute x7, waiting for transfers between devices, partner(): lax.ppermute(value, axis, [(i, i ^ 1 << bit) for i in range(lax.axis_size...  254 us
    all_gather x1, blocking collectives, shards(): lax.all_gather(queries, 'row', axis=0, tiled=True)  23 us
    rev x7, local copies, waits for them, and re-layouts, xor_order(): flipped = shaped[:, ::-1].reshape(slot_data.shape)  18.3 us
    ppermute x7, starting transfers between devices, partner(): lax.ppermute(value, axis, [(i, i ^ 1 << bit) for i in range(lax.axis_size...  14.5 us
    dot_general x1, matrix products, shards(): lax.dot_general(grad_group, weights_lane, (((1,), (1,)), ((), ())), prefe...  14.4 us
    select_n x5, other arithmetic, xor_order(): slot_data = jnp.where(lane_id >> bit_level & 1 == 1, flipped, slot_data)  12.6 us
    select_n x2, other arithmetic, collect(): jnp.where(upper_half, jnp.concatenate([partner_rows, pieces], axis=0), jn...  7.89 us
  transfers between devices with their start and end apart: 7, of which 7 were waited for; matrix products, arithmetic and copies ran while one was open for 1% of the time, Pallas kernels for 0%

commit v1 on v0

--- a/solution.py
+++ b/solution.py
@@ -4,6 +4,18 @@
 from jax.sharding import PartitionSpec as P
 
 SEQ_LEN = 128
+
+
+def gather_by_bits(x, axis, dim):
+    ways, here = (lax.axis_size(axis), lax.axis_index(axis))
+    grown, reach = (x, 1)
+    while reach < ways:
+        theirs = lax.ppermute(grown, axis, [(d, d ^ reach) for d in range(ways)])
+        mine_first = jnp.concatenate([grown, theirs], axis=dim)
+        theirs_first = jnp.concatenate([theirs, grown], axis=dim)
+        grown = jnp.where(here & reach == 0, mine_first, theirs_first)
+        reach = 2 * reach
+    return grown
 
 
 def partner(value, axis, bit):
@@ -99,7 +111,7 @@
     stored_rows = stored.shape[0]
     column = position * stored_rows + jnp.arange(stored_rows, dtype=jnp.int32)
     products = lax.dot_general(
-        lax.all_gather(queries, "row", axis=0, tiled=True),
+        gather_by_bits(queries, "row", 0),
         stored,
         (((1,), (1,)), ((), ())),
         preferred_element_type=jnp.float32,

time: 382 us -> 374 us (0.979)
  blocking collectives: 23 us -> 0 us
  waiting for transfers between devices: 254 us -> 263 us
  starting transfers between devices: 14.5 us -> 21.1 us
    all_gather x1 -> x0, blocking collectives: 23 us -> none  [shards(): lax.all_gather(queries, 'row', axis=0, tiled=True)]
    ppermute x0 -> x4, waiting for transfers between devices: none -> 8.37 us  [gather_by_bits(): theirs = lax.ppermute(grown, axis, [(d, d ^ reach) for d in range(ways)])]
    ppermute x0 -> x4, starting transfers between devices: none -> 6.61 us  [gather_by_bits(): theirs = lax.ppermute(grown, axis, [(d, d ^ reach) for d in range(ways)])]
  transfers between devices with their start and end apart: 7 -> 11, of which waited for: 7 -> 11; matrix products, arithmetic and copies ran while one was open for 1% -> 1% of each run, Pallas kernels for 0% -> 0%
where the time goes in v1:
time: 374 us; the launch traced here: 373 us
  waiting for transfers between devices  263 us (70%)
  local copies, waits for them, and re-layouts  40.8 us (11%)
  other arithmetic  24.5 us (7%)
  matrix products  23.7 us (6%)
  starting transfers between devices  21.1 us (6%)
    ppermute x7, waiting for transfers between devices, partner(): lax.ppermute(value, axis, [(i, i ^ 1 << bit) for i in range(lax.axis_size...  254 us
    rev x7, local copies, waits for them, and re-layouts, xor_order(): flipped = shaped[:, ::-1].reshape(slot_data.shape)  18.3 us
    ppermute x7, starting transfers between devices, partner(): lax.ppermute(value, axis, [(i, i ^ 1 << bit) for i in range(lax.axis_size...  14.5 us
    dot_general x1, matrix products, shards(): lax.dot_general(grad_group, weights_lane, (((1,), (1,)), ((), ())), prefe...  14.4 us
    select_n x5, other arithmetic, xor_order(): slot_data = jnp.where(lane_id >> bit_level & 1 == 1, flipped, slot_data)  12.6 us
    ppermute x4, waiting for transfers between devices, gather_by_bits(): theirs = lax.ppermute(grown, axis, [(d, d ^ reach) for d in range(ways)])  8.37 us
    select_n x2, other arithmetic, collect(): jnp.where(upper_half, jnp.concatenate([partner_rows, pieces], axis=0), jn...  7.88 us
  transfers between devices with their start and end apart: 11, of which 11 were waited for; matrix products, arithmetic and copies ran while one was open for 1% of the time, Pallas kernels for 0%

profile of v1, /device:TPU:0, one launch (start us, length us, event | category | flops | bytes accessed | tf_op | source)
XLA Modules:
  0.0 373.4 jit_solution(16664685154786710187)
XLA Ops:
  0.0 0.0 copy-start
  0.0 0.5 collective-permute-start
  0.5 2.6 collective-permute-done
  3.1 3.1 maximum_select_fusion.5
  6.2 2.9 collective-permute-start.1
  9.2 46.0 %collective-permute-done.1 = bf16[256,4096]{1,0:T(8,128)(2,1)} collective-permute-done((bf16[256,4096]{1,0:T(8,128)(2,1)S(1)}, bf16[256,4096]{1,0:T(8,128)(2,1)}, u32[]{:S(2)}, u32[]{:S(2)}) %collective-permute-start.1) | collective-permute-done | bytes 2097184 | tf_op jit(solution)/shard_map/ppermute | solution.py:22
  55.2 4.7 %maximum_select_fusion.4 = bf16[512,4096]{1,0:T(8,128)(2,1)} fusion(bf16[256,4096]{1,0:T(8,128)(2,1)S(1)} %maximum_select_fusion.5, bf16[256,4096]{1,0:T(8,128)(2,1)} %collective-permute-done.1, pred[]{:T(512)S(6)} %eq.46), kind=kLoop, calls=%fused_computation.17 | loop fusion | flops 18874368 | bytes 8388609 | tf_op jit(solution)/shard_map/jit(_where)/select_n | solution.py:29
  59.9 1.8 collective-permute-start.2
  61.8 2.6 collective-permute-start.3
  64.4 165.7 %collective-permute-done.3 = bf16[448,4096]{1,0:T(8,128)(2,1)} collective-permute-done((bf16[448,4096]{1,0:T(8,128)(2,1)}, bf16[448,4096]{1,0:T(8,128)(2,1)}, u32[]{:S(2)}, u32[]{:S(2)}) %collective-permute-start.3) | collective-permute-done | bytes 3670048 | tf_op jit(solution)/shard_map/ppermute | solution.py:22
  230.0 1.0 collective-permute-done.2
  231.0 14.4 %fusion.20 = bf16[1024,896]{1,0:T(8,128)(2,1)S(1)} fusion(bf16[448,4096]{1,0:T(8,128)(2,1)} %param.11, bf16[448,4096]{1,0:T(8,128)(2,1)} %collective-permute-done.3, pred[]{:T(512)S(6)} %eq.48, bf16[512,4096]{1,0:T(8,128)(2,1)} %maximum_select_fusion.4, bf16[512,4096]{1,0:T(8,128)(2,1)} %collective-permute-done.2, pred[]{:T(512)S(6)} %eq.45), kind=kOutput, calls=%fused_computation.35 | convolution fusion | flops 7587889152 | bytes 17563650 | tf_op jit(solution)/shard_map/dot_general | solution.py:86
  245.4 1.5 rev.18
  246.9 3.6 copy.15
  250.5 2.4 copy.16
  252.9 3.0 broadcast_select_fusion
  255.9 2.9 rev.19
  258.8 2.4 copy.18
  261.2 3.0 select_select_fusion.2
  264.2 2.9 rev.20
  267.1 3.6 copy.20
  270.7 3.6 copy.19
  274.3 0.8 select_select_fusion.1
  275.1 1.1 fusion.41
  276.2 0.0 collective-permute-start.4
  276.2 0.6 copy.21
  276.8 2.2 collective-permute-done.4
  279.0 1.6 copy.22
  280.6 0.2 fusion.28
  280.7 3.5 collective-permute-start.5
  284.3 20.7 %collective-permute-done.5 = bf16[2,2,128,896]{2,3,1,0:T(8,128)(2,1)S(1)} collective-permute-done((bf16[2,2,128,896]{2,3,1,0:T(8,128)(2,1)S(1)}, bf16[2,2,128,896]{2,3,1,0:T(8,128)(2,1)S(1)}, u32[]{:S(2)}, u32[]{:S(2)}) %collective-permute-start.5) | collective-permute-done | bytes 917536 | tf_op jit(solution)/shard_map/ppermute | solution.py:22
  304.9 0.2 pad_maximum_fusion
  305.1 1.0 fusion.40
  306.1 3.2 collective-permute-start.6
  309.3 3.9 %copy.25 = bf16[128,7168]{0,1:T(8,128)(2,1)} copy(bf16[128,7168]{1,0:T(8,128)(2,1)} %param.9) | data formatting | bytes 3670016 | tf_op args[1]
  313.2 0.0 copy-done
  313.2 0.0 copy-done.4
  313.2 0.4 convolution_convert_fusion
  313.6 16.0 %collective-permute-done.6 = bf16[1,4,128,896]{2,3,1,0:T(8,128)(2,1)S(1)} collective-permute-done((bf16[1,4,128,896]{2,3,1,0:T(8,128)(2,1)}, bf16[1,4,128,896]{2,3,1,0:T(8,128)(2,1)S(1)}, u32[]{:S(2)}, u32[]{:S(2)}) %collective-permute-start.6) | collective-permute-done | bytes 917536 | tf_op jit(solution)/shard_map/ppermute | solution.py:22
  329.6 0.0 copy-done.1
  329.6 1.6 pad_maximum_fusion.1
  331.2 0.0 copy-done.2
  331.2 1.6 rev.21
  332.8 2.9 maximum_select_fusion.6
  335.8 2.9 rev.22
  338.7 2.9 select_select_fusion
  341.6 2.9 rev.23
  344.6 1.8 select_bitcast_fusion
  346.4 1.4 copy.24
  347.8 0.8 copy-done.3
  348.6 3.7 multiply_reduce_fusion
  353.0 0.1 convert_element_type.41
  353.1 0.0 collective-permute-start.7
  353.1 1.2 collective-permute-done.7
  354.3 0.1 broadcast_select_fusion.1
  354.4 2.6 collective-permute-start.8
  356.9 1.7 collective-permute-done.8
  358.7 0.1 maximum_select_fusion.14
  358.7 2.4 collective-permute-start.9
  361.1 1.9 collective-permute-done.9
  363.0 0.1 maximum_select_fusion.13
  363.1 1.6 collective-permute-start.10
  364.7 3.6 collective-permute-done.10
  368.3 5.1 %convolution_select_fusion = f32[16,768]{1,0:T(8,128)} fusion(bf16[768,4096]{1,0:T(8,128)(2,1)} %param.14, bf16[8,4096]{1,0:T(8,128)(2,1)S(1)} %collective-permute-done.10, bf16[8,4096]{1,0:T(8,128)(2,1)S(1)} %maximum_select_fusion.13, pred[]{:T(512)S(6)} %eq.38, s32[768]{0:T(1024)S(1)} %iota_add_fusion, s32[16]{0:T(128)S(1)} %copy-done.5), kind=kOutput, calls=%fused_computation.37 | convolution fusion | flops 101277696 | bytes 6474817 | tf_op jit(solution)/shard_map/dot_general | solution.py:113
  (8 shorter events, 0.0 us)
Async XLA Ops:
  0.0 313.2 %copy-start = (bf16[128,4096]{1,0:T(8,128)(2,1)S(1)}, bf16[128,4096]{1,0:T(8,128)(2,1)}, u32[]{:S(2)}) copy-start(bf16[128,4096]{1,0:T(8,128)(2,1)} %param.8) | copy-start | bytes 3145732
  0.0 3.1 collective-permute-start
  6.2 49.0 %collective-permute-start.1 = (bf16[256,4096]{1,0:T(8,128)(2,1)S(1)}, bf16[256,4096]{1,0:T(8,128)(2,1)}, u32[]{:S(2)}, u32[]{:S(2)}) collective-permute-start(bf16[256,4096]{1,0:T(8,128)(2,1)S(1)} %maximum_select_fusion.5), channel_id=1, source_target_pairs={{0,2},{1,3},{2,0},{3,1},{4,6},{5,7},{6,4},{7,5},{8,10},{9,11},{10,... | collective-permute-start | bytes 6291464 | tf_op jit(solution)/shard_map/ppermute | solution.py:22
  59.9 171.1 %collective-permute-start.2 = (bf16[512,4096]{1,0:T(8,128)(2,1)}, bf16[512,4096]{1,0:T(8,128)(2,1)}, u32[]{:S(2)}, u32[]{:S(2)}) collective-permute-start(bf16[512,4096]{1,0:T(8,128)(2,1)} %maximum_select_fusion.4), channel_id=1, source_target_pairs={{0,4},{1,5},{2,6},{3,7},{4,0},{5,1},{6,2},{7,3},{8,12},{9,13},{10,... | collective-permute-start | bytes 12582920 | tf_op jit(solution)/shard_map/ppermute | solution.py:22
  61.8 168.3 %collective-permute-start.3 = (bf16[448,4096]{1,0:T(8,128)(2,1)}, bf16[448,4096]{1,0:T(8,128)(2,1)}, u32[]{:S(2)}, u32[]{:S(2)}) collective-permute-start(bf16[448,4096]{1,0:T(8,128)(2,1)} %param.11), channel_id=1, source_target_pairs={{0,8},{1,9},{2,10},{3,11},{4,12},{5,13},{6,14},{7,15},{8,0},{9,1},... | collective-permute-start | bytes 11010056 | tf_op jit(solution)/shard_map/ppermute | solution.py:22
  276.2 2.8 collective-permute-start.4
  280.7 24.2 %collective-permute-start.5 = (bf16[2,2,128,896]{2,3,1,0:T(8,128)(2,1)S(1)}, bf16[2,2,128,896]{2,3,1,0:T(8,128)(2,1)S(1)}, u32[]{:S(2)}, u32[]{:S(2)}) collective-permute-start(bf16[2,2,128,896]{2,3,1,0:T(8,128)(2,1)S(1)} %get-tuple-element.8), channel_id=1, source_target_pairs={{0,2},{1,3},{2,0},{3,1},{4,6},{5,7},{6,4},{7,5},{8,10},{9,11},{10,... | collective-permute-start | bytes 2752520 | tf_op jit(solution)/shard_map/ppermute | solution.py:22
  306.1 23.5 %copy-start.1 = (bf16[1,1,4,128,896]{3,4,2,1,0:T(8,128)(2,1)}, bf16[1,1,4,128,896]{3,4,2,1,0:T(8,128)(2,1)S(1)}, u32[]{:S(2)}) copy-start(bf16[1,1,4,128,896]{3,4,2,1,0:T(8,128)(2,1)S(1)} %get-tuple-element.5) | copy-start | bytes 2752516
  306.1 7.0 %copy-start.4 = (bf16[4096,64]{0,1:T(8,128)(2,1)S(1)}, bf16[4096,64]{0,1:T(8,128)(2,1)}, u32[]{:S(2)}) copy-start(bf16[4096,64]{0,1:T(8,128)(2,1)} %param.12) | copy-start | bytes 1572868
  306.1 23.5 %collective-permute-start.6 = (bf16[1,4,128,896]{2,3,1,0:T(8,128)(2,1)}, bf16[1,4,128,896]{2,3,1,0:T(8,128)(2,1)S(1)}, u32[]{:S(2)}, u32[]{:S(2)}) collective-permute-start(bf16[1,4,128,896]{2,3,1,0:T(8,128)(2,1)} %get-tuple-element.6), channel_id=1, source_target_pairs={{0,4},{1,5},{2,6},{3,7},{4,0},{5,1},{6,2},{7,3},{8,12},{9,13},{10,... | collective-permute-start | bytes 2752520 | tf_op jit(solution)/shard_map/ppermute | solution.py:22
  329.6 1.6 copy-start.2
  346.4 2.2 copy-start.3
  348.6 19.7 %copy-start.5 = (s32[16]{0:T(128)S(1)}, s32[16]{0:T(128)}, u32[]{:S(2)}) copy-start(s32[16]{0:T(128)} %param.15) | copy-start | bytes 196
  353.1 1.2 collective-permute-start.7
  354.4 4.3 %collective-permute-start.8 = (bf16[2,4096]{1,0:T(2,128)(2,1)S(1)}, bf16[2,4096]{1,0:T(2,128)(2,1)S(1)}, u32[]{:S(2)}, u32[]{:S(2)}) collective-permute-start(bf16[2,4096]{1,0:T(2,128)(2,1)S(1)} %broadcast_select_fusion.1), channel_id=1, source_target_pairs={{0,2},{1,3},{2,0},{3,1},{4,6},{5,7},{6,4},{7,5},{8,10},{9,11},{10,... | collective-permute-start | bytes 49160 | tf_op jit(solution)/shard_map/ppermute | solution.py:13
  358.7 4.3 %collective-permute-start.9 = (bf16[4,4096]{1,0:T(4,128)(2,1)S(1)}, bf16[4,4096]{1,0:T(4,128)(2,1)S(1)}, u32[]{:S(2)}, u32[]{:S(2)}) collective-permute-start(bf16[4,4096]{1,0:T(4,128)(2,1)S(1)} %maximum_select_fusion.14), channel_id=1, source_target_pairs={{0,4},{1,5},{2,6},{3,7},{4,0},{5,1},{6,2},{7,3},{8,12},{9,13},{10,... | collective-permute-start | bytes 98312 | tf_op jit(solution)/shard_map/ppermute | solution.py:13
  363.1 5.2 %collective-permute-start.10 = (bf16[8,4096]{1,0:T(8,128)(2,1)S(1)}, bf16[8,4096]{1,0:T(8,128)(2,1)S(1)}, u32[]{:S(2)}, u32[]{:S(2)}) collective-permute-start(bf16[8,4096]{1,0:T(8,128)(2,1)S(1)} %maximum_select_fusion.13), channel_id=1, source_target_pairs={{0,8},{1,9},{2,10},{3,11},{4,12},{5,13},{6,14},{7,15},{8,0},{9,1},... | collective-permute-start | bytes 196616 | tf_op jit(solution)/shard_map/ppermute | solution.py:13
